TPU v7x, 32 devices: a whole 2x2x4 slice. The times are simulated.
32 devices in a mesh: dp: 8 (over z, core), fsdp: 4 (over y, x).
Axes of the slice: x: 2, y: 2, z: 4, core: 2. Of those that a mesh axis runs over, the one named last changes fastest.
Arguments:
- tokens: bfloat16 [32, 1024, 768], P(('dp', 'fsdp')), may hold values from -6 to 6
- lengths: int32 [32], P(('dp', 'fsdp')), may hold values from 1 to 1024, as said below
- keep_attn: int32 [32, 1024, 768], P(('dp', 'fsdp')), may hold values 0 or 1
- keep_ffn: int32 [32, 1024, 768], P(('dp', 'fsdp')), may hold values 0 or 1
- partners: int32 [32], replicated, may hold values from 0 to 31, as said below
- out_cot: bfloat16 [32, 1024, 768], P(('dp', 'fsdp')), may hold values from -6 to 6
- w_qkv: bfloat16 [768, 2304], P(('dp', 'fsdp')), may hold values from -0.21875 to 0.21875
- b_qv: bfloat16 [1536], P(('dp', 'fsdp')), may hold values from -3 to 3
- w_out: bfloat16 [768, 768], P(('dp', 'fsdp')), may hold values from -6 to 6
- b_out: bfloat16 [768], P(('dp', 'fsdp')), may hold values from -3 to 3
- ln1_gain: bfloat16 [768], P(('dp', 'fsdp')), may hold values from 0.099609375 to 1.8984375
- ln1_bias: bfloat16 [768], P(('dp', 'fsdp')), may hold values from -3 to 3
- w_up: bfloat16 [768, 3072], P(('dp', 'fsdp')), may hold values from -0.21875 to 0.21875
- b_up: bfloat16 [3072], P(('dp', 'fsdp')), may hold values from -3 to 3
- w_down: bfloat16 [3072, 768], P(('dp', 'fsdp')), may hold values from -0.109375 to 0.109375
- b_down: bfloat16 [768], P(('dp', 'fsdp')), may hold values from -3 to 3
- ln2_gain: bfloat16 [768], P(('dp', 'fsdp')), may hold values from 0.099609375 to 1.8984375
- ln2_bias: bfloat16 [768], P(('dp', 'fsdp')), may hold values from -3 to 3
- w_pool: bfloat16 [768, 768], P(('dp', 'fsdp')), may hold values from -0.21875 to 0.21875
- b_pool: bfloat16 [768], P(('dp', 'fsdp')), may hold values from -3 to 3
Outputs:
- layer_out: bfloat16 [32, 1024, 768], P(('dp', 'fsdp'))
- tokens_grad: bfloat16 [32, 1024, 768], P(('dp', 'fsdp'))
- grad_w_qkv: float32 [768, 2304], P(('dp', 'fsdp'))
- grad_b_qv: float32 [1536], P(('dp', 'fsdp'))
- grad_w_out: float32 [768, 768], P(('dp', 'fsdp'))
- grad_b_out: float32 [768], P(('dp', 'fsdp'))
- grad_ln1_gain: float32 [768], P(('dp', 'fsdp'))
- grad_ln1_bias: float32 [768], P(('dp', 'fsdp'))
- grad_w_up: float32 [768, 3072], P(('dp', 'fsdp'))
- grad_b_up: float32 [3072], P(('dp', 'fsdp'))
- grad_w_down: float32 [3072, 768], P(('dp', 'fsdp'))
- grad_b_down: float32 [768], P(('dp', 'fsdp'))
- grad_ln2_gain: float32 [768], P(('dp', 'fsdp'))
- grad_ln2_bias: float32 [768], P(('dp', 'fsdp'))
- grad_w_pool: float32 [768, 768], P(('dp', 'fsdp'))
- grad_b_pool: float32 [768], P(('dp', 'fsdp'))
- loss: float32 [], replicated
Inputs may be any that keep to these rules, and one draw needn't show every extreme that they name: partners[partners[i]] = i and partners[i] != i: the 32 views form 32 / 2 pairs. lengths[partners[i]] = lengths[i]; the longest view has exactly 1024 live tokens.
All inputs are finite; a program needn't handle non-finite values. No bound on the sum of `keep_attn` or of `keep_ffn` on one device may be relied on, other than what follows from the above.
Results may differ from a plain program's by a relative error of at most 0.029.
Values may be sent and summed in bfloat16 or wider, within the bound.
A program may use at most 256 MiB of HBM per device.

v0:
```python
import functools
import math

import jax
import jax.numpy as jnp
from jax import lax
from jax.sharding import PartitionSpec as P

HEAD_DIM = 64


full_accuracy_setting = lax.Precision.HIGHEST
eps_norm = 1e-05
keep_scale = 1.0 / 0.9
logit_divisor = 0.05
neg_fill = -1000000000.0


def layer_norm(values, gain, shift):
    center = values - jnp.mean(values, axis=-1, keepdims=True)
    spread = jnp.mean(center * center, axis=-1, keepdims=True)
    return center * lax.rsqrt(spread + eps_norm) * gain + shift


def gelu_exact(values):
    return 0.5 * values * (1.0 + lax.erf(values * (1.0 / math.sqrt(2.0))))


def contrast_loss(pooled, partners):
    unit_length_embeddings = pooled * lax.rsqrt(
        jnp.sum(pooled * pooled, axis=1, keepdims=True) + 1e-06
    )
    angle_similarity_table = (
        jnp.dot(unit_length_embeddings, unit_length_embeddings.T, precision=full_accuracy_setting)
        / logit_divisor
    )
    count = pooled.shape[0]
    columns = jnp.arange(count, dtype=jnp.int32)
    others = jnp.where(columns[:, None] == columns[None, :], neg_fill, angle_similarity_table)
    row_max = jnp.max(others, axis=1, keepdims=True)
    log_total = row_max[:, 0] + jnp.log(jnp.sum(jnp.exp(others - row_max), axis=1))
    target = jnp.sum(
        jnp.where(partners[:, None] == columns[None, :], angle_similarity_table, 0.0), axis=1
    )
    return jnp.mean(log_total - target)


def block_scores(query_block, key_rows, valid_keys):
    score_scale = 1.0 / math.sqrt(query_block.shape[-1])
    raw = (
        jnp.einsum("qhd,khd->hqk", query_block, key_rows, preferred_element_type=jnp.float32)
        * score_scale
    )
    return jnp.where(valid_keys[None, None, :], raw, neg_fill)


def attention_forward(query_rows, key_rows, value_rows, lengths):
    num_seqs, length, num_heads, head_width = query_rows.shape
    block_rows = min(512, length)
    num_blocks = length // block_rows

    def per_seq(inputs_one):
        seq_query, seq_keys, sequence_value_rows, seq_length = inputs_one
        valid_keys = jnp.arange(length, dtype=jnp.int32) < seq_length

        def per_block(query_block):
            scores = block_scores(query_block, seq_keys, valid_keys)
            row_max = jnp.max(scores, axis=2, keepdims=True)
            shifted = jnp.exp(scores - row_max)
            row_total = jnp.sum(shifted, axis=2, keepdims=True)
            probabilities = (shifted / row_total).astype(jnp.bfloat16)
            context = jnp.einsum(
                "hqk,khd->qhd",
                probabilities,
                sequence_value_rows,
                preferred_element_type=jnp.float32,
            )
            return (context.astype(jnp.bfloat16), (row_max + jnp.log(row_total))[:, :, 0])

        context, log_total = lax.map(
            per_block, seq_query.reshape(num_blocks, block_rows, num_heads, head_width)
        )
        return (context.reshape(length, num_heads * head_width), log_total)

    return lax.map(per_seq, (query_rows, key_rows, value_rows, lengths))


def attention_backward(query_rows, key_rows, value_rows, context_grad, log_total, lengths):
    num_seqs, length, num_heads, head_width = query_rows.shape
    block_rows = min(512, length)
    num_blocks = length // block_rows
    score_scale = 1.0 / math.sqrt(head_width)

    def per_seq(inputs_one):
        seq_query, seq_keys, sequence_value_rows, seq_grad, seq_total, seq_length = inputs_one
        valid_keys = jnp.arange(length, dtype=jnp.int32) < seq_length

        def per_block(carried, block_in):
            key_acc, value_acc = carried
            query_block, grad_block, total_block = block_in
            scores = block_scores(query_block, seq_keys, valid_keys)
            probabilities = jnp.exp(scores - total_block[:, :, None])
            prob_grad = jnp.einsum(
                "qhd,khd->hqk", grad_block, sequence_value_rows, preferred_element_type=jnp.float32
            )
            inner_sum = jnp.sum(probabilities * prob_grad, axis=2, keepdims=True)
            score_grad = (probabilities * (prob_grad - inner_sum)).astype(jnp.bfloat16)
            value_acc = value_acc + jnp.einsum(
                "hqk,qhd->khd",
                probabilities.astype(jnp.bfloat16),
                grad_block,
                preferred_element_type=jnp.float32,
            )
            key_acc = (
                key_acc
                + jnp.einsum(
                    "hqk,qhd->khd", score_grad, query_block, preferred_element_type=jnp.float32
                )
                * score_scale
            )
            query_grad = (
                jnp.einsum("hqk,khd->qhd", score_grad, seq_keys, preferred_element_type=jnp.float32)
                * score_scale
            )
            return ((key_acc, value_acc), query_grad)

        zeros_kv = jnp.zeros((length, num_heads, head_width), jnp.float32)
        (key_grad, value_grad), query_grad = lax.scan(
            per_block,
            (zeros_kv, zeros_kv),
            (
                seq_query.reshape(num_blocks, block_rows, num_heads, head_width),
                seq_grad.reshape(num_blocks, block_rows, num_heads, head_width),
                seq_total,
            ),
        )
        model_width = num_heads * head_width
        return (
            query_grad.reshape(length, model_width),
            key_grad.reshape(length, model_width),
            value_grad.reshape(length, model_width),
        )

    return lax.map(per_seq, (query_rows, key_rows, value_rows, context_grad, log_total, lengths))


def local_forward(tokens, lengths, keep_attn, keep_ffn, gathered):
    (
        w_qkv,
        b_qv,
        w_out,
        b_out,
        ln1_gain,
        ln1_bias,
        w_up,
        b_up,
        w_down,
        b_down,
        ln2_gain,
        ln2_bias,
        w_pool,
        b_pool,
    ) = gathered
    num_seqs, length, model_width = tokens.shape
    num_heads = model_width // HEAD_DIM
    flat_rows = tokens.reshape(num_seqs * length, model_width)
    projected = jnp.dot(flat_rows, w_qkv, preferred_element_type=jnp.float32)
    query_key_value_bias = jnp.concatenate(
        [b_qv[:model_width], jnp.zeros((model_width,), jnp.bfloat16), b_qv[model_width:]]
    ).astype(jnp.float32)
    projected = (projected + query_key_value_bias).astype(jnp.bfloat16)
    shape_four = (num_seqs, length, num_heads, HEAD_DIM)
    query_rows = projected[:, :model_width].reshape(shape_four)
    key_rows = projected[:, model_width : 2 * model_width].reshape(shape_four)
    value_rows = projected[:, 2 * model_width :].reshape(shape_four)
    context, log_total = attention_forward(query_rows, key_rows, value_rows, lengths)
    context = context.reshape(num_seqs * length, model_width)
    attended = jnp.dot(context, w_out, preferred_element_type=jnp.float32) + b_out.astype(
        jnp.float32
    )
    keep_a = keep_attn.reshape(-1, model_width).astype(jnp.float32) * keep_scale
    keep_f = keep_ffn.reshape(-1, model_width).astype(jnp.float32) * keep_scale
    first_sum = flat_rows.astype(jnp.float32) + attended * keep_a
    hidden = layer_norm(first_sum, ln1_gain.astype(jnp.float32), ln1_bias.astype(jnp.float32))
    hidden_low = hidden.astype(jnp.bfloat16)
    up_pre = jnp.dot(hidden_low, w_up, preferred_element_type=jnp.float32) + b_up.astype(
        jnp.float32
    )
    activated = gelu_exact(up_pre).astype(jnp.bfloat16)
    down_out = jnp.dot(activated, w_down, preferred_element_type=jnp.float32) + b_down.astype(
        jnp.float32
    )
    second_sum = hidden + down_out * keep_f
    normed_out = layer_norm(second_sum, ln2_gain.astype(jnp.float32), ln2_bias.astype(jnp.float32))
    leading_token_states = normed_out.reshape(num_seqs, length, model_width)[:, 0, :].astype(
        jnp.bfloat16
    )
    pooled = jnp.tanh(
        jnp.dot(leading_token_states, w_pool, preferred_element_type=jnp.float32)
        + b_pool.astype(jnp.float32)
    )
    return {
        "flat_rows": flat_rows,
        "query_rows": query_rows,
        "key_rows": key_rows,
        "value_rows": value_rows,
        "context": context,
        "log_total": log_total,
        "keep_a": keep_a,
        "keep_f": keep_f,
        "first_sum": first_sum,
        "hidden_low": hidden_low,
        "up_pre": up_pre,
        "activated": activated,
        "second_sum": second_sum,
        "normed_out": normed_out,
        "cls_rows": leading_token_states,
        "pooled": pooled,
    }


def on_device(
    tokens,
    lengths,
    keep_attn,
    keep_ffn,
    partners,
    out_cot,
    w_qkv,
    b_qv,
    w_out,
    b_out,
    ln1_gain,
    ln1_bias,
    w_up,
    b_up,
    w_down,
    b_down,
    ln2_gain,
    ln2_bias,
    w_pool,
    b_pool,
):
    shards = (
        w_qkv,
        b_qv,
        w_out,
        b_out,
        ln1_gain,
        ln1_bias,
        w_up,
        b_up,
        w_down,
        b_down,
        ln2_gain,
        ln2_bias,
        w_pool,
        b_pool,
    )
    num_seqs, length, model_width = tokens.shape
    gathered = (
        lax.all_gather(w_qkv, ("dp", "fsdp"), axis=0, tiled=True),
        lax.all_gather(b_qv, ("dp", "fsdp"), axis=0, tiled=True),
        lax.all_gather(w_out, ("dp", "fsdp"), axis=0, tiled=True),
        lax.all_gather(b_out, ("dp", "fsdp"), axis=0, tiled=True),
        lax.all_gather(ln1_gain, ("dp", "fsdp"), axis=0, tiled=True),
        lax.all_gather(ln1_bias, ("dp", "fsdp"), axis=0, tiled=True),
        lax.all_gather(w_up, ("dp", "fsdp"), axis=0, tiled=True),
        lax.all_gather(b_up, ("dp", "fsdp"), axis=0, tiled=True),
        lax.all_gather(w_down, ("dp", "fsdp"), axis=0, tiled=True),
        lax.all_gather(b_down, ("dp", "fsdp"), axis=0, tiled=True),
        lax.all_gather(ln2_gain, ("dp", "fsdp"), axis=0, tiled=True),
        lax.all_gather(ln2_bias, ("dp", "fsdp"), axis=0, tiled=True),
        lax.all_gather(w_pool, ("dp", "fsdp"), axis=0, tiled=True),
        lax.all_gather(b_pool, ("dp", "fsdp"), axis=0, tiled=True),
    )
    forward_state = local_forward(tokens, lengths, keep_attn, keep_ffn, gathered)
    layer_out = (
        forward_state["normed_out"].astype(jnp.bfloat16).reshape(num_seqs, length, model_width)
    )
    pooled_all = lax.all_gather(forward_state["pooled"], ("dp", "fsdp"), axis=0, tiled=True)
    loss, loss_pull = jax.vjp(functools.partial(contrast_loss, partners=partners), pooled_all)
    (pooled_grad_all,) = loss_pull(jnp.asarray(pooled_all.shape[0], jnp.float32))
    pooled_grad = lax.dynamic_slice_in_dim(
        pooled_grad_all, lax.axis_index(("dp", "fsdp")) * num_seqs, num_seqs, 0
    )
    weights_back = (
        lax.all_gather(shards[0], ("dp", "fsdp"), axis=0, tiled=True),
        lax.all_gather(shards[1], ("dp", "fsdp"), axis=0, tiled=True),
        lax.all_gather(shards[2], ("dp", "fsdp"), axis=0, tiled=True),
        lax.all_gather(shards[3], ("dp", "fsdp"), axis=0, tiled=True),
        lax.all_gather(shards[4], ("dp", "fsdp"), axis=0, tiled=True),
        lax.all_gather(shards[5], ("dp", "fsdp"), axis=0, tiled=True),
        lax.all_gather(shards[6], ("dp", "fsdp"), axis=0, tiled=True),
        lax.all_gather(shards[7], ("dp", "fsdp"), axis=0, tiled=True),
        lax.all_gather(shards[8], ("dp", "fsdp"), axis=0, tiled=True),
        lax.all_gather(shards[9], ("dp", "fsdp"), axis=0, tiled=True),
        lax.all_gather(shards[10], ("dp", "fsdp"), axis=0, tiled=True),
        lax.all_gather(shards[11], ("dp", "fsdp"), axis=0, tiled=True),
        lax.all_gather(shards[12], ("dp", "fsdp"), axis=0, tiled=True),
        lax.all_gather(shards[13], ("dp", "fsdp"), axis=0, tiled=True),
    )
    kept_state = local_forward(tokens, lengths, keep_attn, keep_ffn, weights_back)
    (
        w_qkv_all,
        b_qv_all,
        w_out_all,
        b_out_all,
        ln1_gain_all,
        first_layernorm_offsets,
        w_up_all,
        b_up_all,
        w_down_all,
        down_bias_stack,
        ln2_gain_all,
        ln2_bias_all,
        w_pool_all,
        b_pool_all,
    ) = weights_back
    pooled = kept_state["pooled"]
    pre_grad = (pooled_grad * (1.0 - pooled * pooled)).astype(jnp.bfloat16)
    pool_weight_grad = jnp.dot(
        kept_state["cls_rows"].T, pre_grad, preferred_element_type=jnp.float32
    )
    pool_bias_grad = jnp.sum(pre_grad, axis=0, dtype=jnp.float32)
    cls_grad = jnp.dot(pre_grad, w_pool_all.T, preferred_element_type=jnp.float32)
    out_grad = out_cot.astype(jnp.float32).at[:, 0, :].add(cls_grad).reshape(-1, model_width)
    _, norm_pull = jax.vjp(
        layer_norm,
        kept_state["second_sum"],
        ln2_gain_all.astype(jnp.float32),
        ln2_bias_all.astype(jnp.float32),
    )
    second_grad, ln2_gain_grad, ln2_bias_grad = norm_pull(out_grad)
    down_grad = (second_grad * kept_state["keep_f"]).astype(jnp.bfloat16)
    down_bias_grad = jnp.sum(down_grad, axis=0, dtype=jnp.float32)
    down_weight_grad = jnp.dot(
        kept_state["activated"].T, down_grad, preferred_element_type=jnp.float32
    )
    activated_grad = jnp.dot(down_grad, w_down_all.T, preferred_element_type=jnp.float32)
    _, gelu_pull = jax.vjp(gelu_exact, kept_state["up_pre"])
    (up_grad,) = gelu_pull(activated_grad)
    up_grad = up_grad.astype(jnp.bfloat16)
    up_bias_grad = jnp.sum(up_grad, axis=0, dtype=jnp.float32)
    up_weight_grad = jnp.dot(
        kept_state["hidden_low"].T, up_grad, preferred_element_type=jnp.float32
    )
    hidden_grad = second_grad + jnp.dot(up_grad, w_up_all.T, preferred_element_type=jnp.float32)
    _, first_pull = jax.vjp(
        layer_norm,
        kept_state["first_sum"],
        ln1_gain_all.astype(jnp.float32),
        first_layernorm_offsets.astype(jnp.float32),
    )
    first_grad, ln1_gain_grad, ln1_bias_grad = first_pull(hidden_grad)
    attended_grad = (first_grad * kept_state["keep_a"]).astype(jnp.bfloat16)
    out_bias_grad = jnp.sum(attended_grad, axis=0, dtype=jnp.float32)
    out_weight_grad = jnp.dot(
        kept_state["context"].T, attended_grad, preferred_element_type=jnp.float32
    )
    context_grad = jnp.dot(attended_grad, w_out_all.T, preferred_element_type=jnp.float32).astype(
        jnp.bfloat16
    )
    query_rows = kept_state["query_rows"]
    query_grad, key_grad, value_grad = attention_backward(
        query_rows,
        kept_state["key_rows"],
        kept_state["value_rows"],
        context_grad.reshape(query_rows.shape),
        kept_state["log_total"],
        lengths,
    )
    token_count = num_seqs * length
    proj_grad = jnp.concatenate(
        [
            query_grad.reshape(token_count, model_width),
            key_grad.reshape(token_count, model_width),
            value_grad.reshape(token_count, model_width),
        ],
        axis=1,
    ).astype(jnp.bfloat16)
    column_sums = jnp.sum(proj_grad, axis=0, dtype=jnp.float32)
    qv_bias_grad = jnp.concatenate([column_sums[:model_width], column_sums[2 * model_width :]])
    qkv_weight_grad = jnp.dot(
        kept_state["flat_rows"].T, proj_grad, preferred_element_type=jnp.float32
    )
    tokens_grad = first_grad + jnp.dot(proj_grad, w_qkv_all.T, preferred_element_type=jnp.float32)
    tokens_grad = tokens_grad.astype(jnp.bfloat16).reshape(num_seqs, length, model_width)
    summed = (
        lax.psum_scatter(qkv_weight_grad, ("dp", "fsdp"), scatter_dimension=0, tiled=True),
        lax.psum_scatter(qv_bias_grad, ("dp", "fsdp"), scatter_dimension=0, tiled=True),
        lax.psum_scatter(out_weight_grad, ("dp", "fsdp"), scatter_dimension=0, tiled=True),
        lax.psum_scatter(out_bias_grad, ("dp", "fsdp"), scatter_dimension=0, tiled=True),
        lax.psum_scatter(ln1_gain_grad, ("dp", "fsdp"), scatter_dimension=0, tiled=True),
        lax.psum_scatter(ln1_bias_grad, ("dp", "fsdp"), scatter_dimension=0, tiled=True),
        lax.psum_scatter(up_weight_grad, ("dp", "fsdp"), scatter_dimension=0, tiled=True),
        lax.psum_scatter(up_bias_grad, ("dp", "fsdp"), scatter_dimension=0, tiled=True),
        lax.psum_scatter(down_weight_grad, ("dp", "fsdp"), scatter_dimension=0, tiled=True),
        lax.psum_scatter(down_bias_grad, ("dp", "fsdp"), scatter_dimension=0, tiled=True),
        lax.psum_scatter(ln2_gain_grad, ("dp", "fsdp"), scatter_dimension=0, tiled=True),
        lax.psum_scatter(ln2_bias_grad, ("dp", "fsdp"), scatter_dimension=0, tiled=True),
        lax.psum_scatter(pool_weight_grad, ("dp", "fsdp"), scatter_dimension=0, tiled=True),
        lax.psum_scatter(pool_bias_grad, ("dp", "fsdp"), scatter_dimension=0, tiled=True),
    )
    return (
        layer_out,
        tokens_grad,
        summed[0],
        summed[1],
        summed[2],
        summed[3],
        summed[4],
        summed[5],
        summed[6],
        summed[7],
        summed[8],
        summed[9],
        summed[10],
        summed[11],
        summed[12],
        summed[13],
        loss,
    )


def solution(mesh):
    in_specs = (
        P(("dp", "fsdp"), None, None),
        P(("dp", "fsdp")),
        P(("dp", "fsdp"), None, None),
        P(("dp", "fsdp"), None, None),
        P(),
        P(("dp", "fsdp"), None, None),
        P(("dp", "fsdp"), None),
        P(("dp", "fsdp")),
        P(("dp", "fsdp"), None),
        P(("dp", "fsdp")),
        P(("dp", "fsdp")),
        P(("dp", "fsdp")),
        P(("dp", "fsdp"), None),
        P(("dp", "fsdp")),
        P(("dp", "fsdp"), None),
        P(("dp", "fsdp")),
        P(("dp", "fsdp")),
        P(("dp", "fsdp")),
        P(("dp", "fsdp"), None),
        P(("dp", "fsdp")),
    )
    out_specs = (
        P(("dp", "fsdp"), None, None),
        P(("dp", "fsdp"), None, None),
        P(("dp", "fsdp"), None),
        P(("dp", "fsdp")),
        P(("dp", "fsdp"), None),
        P(("dp", "fsdp")),
        P(("dp", "fsdp")),
        P(("dp", "fsdp")),
        P(("dp", "fsdp"), None),
        P(("dp", "fsdp")),
        P(("dp", "fsdp"), None),
        P(("dp", "fsdp")),
        P(("dp", "fsdp")),
        P(("dp", "fsdp")),
        P(("dp", "fsdp"), None),
        P(("dp", "fsdp")),
        P(),
    )
    return jax.shard_map(
        on_device, mesh=mesh, in_specs=in_specs, out_specs=out_specs, check_vma=False
    )
```

profile of v0, /device:TPU:0, one launch (start us, length us, event | category | flops | bytes accessed | tf_op | source)
XLA Modules:
  0.0 1064.3 jit_solution(6393665988555967279)
XLA Ops:
  18.2 42.8 %all-reduce.19 = (bf16[1536]{0:T(1024)(128)(2,1)S(1)}, bf16[768]{0:T(1024)(128)(2,1)S(1)}, bf16[3072]{0:T(1024)(128)(2,1)S(1)}, bf16[768]{0:T(1024)(128)(2,1)S(1...) all-reduce(bf16[1536]{0:T(1024)(128)(2,1)S(1)} %dynamic-update-slic, ...), channel_id=1, replica_groups=mesh['dp'=8,'fsdp'=4] {'dp','fsdp'}, use_global_device_ids=true, to_apply=%add | all-reduce | flops 9984 | bytes 39936
  93.5 69.4 %while.68 = (s32[]{:T(128)}, bf16[2,512,12,64]{1,3,2,0:T(8,128)(2,1)}, f32[2,12,512]{2,1,0:T(8,128)S(1)}, bf16[2,512,12,64]{1,3,2,0:T(8,128)(2,1)S(1)}, bf16[102...) while((s32[]{:T(128)}, ...), condition=%wide.region_17.18_spmd.clone, body=%wide.region_14.17_spmd.clone.sunk | while | flops 1686498304 | bytes 99332296 | solution.py:80
  104.3 11.4 %fusion.191 = f32[12,512]{1,0:T(8,128)S(1)} fusion(f32[12,512,1024]{2,1,0:T(8,128)} %get-tuple-element.672, f32[12,512]{1,0:T(8,128)S(1)} %get-tuple-element.673, pred[1024]{0:T(1024)(128)(4,1)S(1)} %iota_compare_fusion.9), kind=kLoop, calls=%fused_computation.26.clone.1 | loop fusion | flops 25159680 | bytes 25216000 | tf_op jit(solution)/shard_map/while/body/eval_jaxpr/while/body/eval_jaxpr/reduce_sum | solution.py:70
  138.9 11.5 %fusion.191 = f32[12,512]{1,0:T(8,128)S(1)} fusion(f32[12,512,1024]{2,1,0:T(8,128)} %get-tuple-element.672, f32[12,512]{1,0:T(8,128)S(1)} %get-tuple-element.673, pred[1024]{0:T(1024)(128)(4,1)S(1)} %iota_compare_fusion.9), kind=kLoop, calls=%fused_computation.26.clone.1 | loop fusion | flops 25159680 | bytes 25216000 | tf_op jit(solution)/shard_map/while/body/eval_jaxpr/while/body/eval_jaxpr/reduce_sum | solution.py:70
  150.4 11.3 %fusion.192 = bf16[2,512,12,64]{1,3,2,0:T(8,128)(2,1)S(1)} fusion(bf16[2,512,12,64]{1,3,2,0:T(8,128)(2,1)S(1)} %copy-done.15, s32[]{:T(128)S(6)} %copy.119, bf16[1024,12,64]{0,2,1:T(8,128)(2,1)S(1)} %copy-done.1, f32[12,512,1024]{2,1,0:T(8,128)} %get-tuple-element.672, f32[12,512]{1,0:T(8,128)S(1)} %fusion.191, ...), kind=kOutput, calls=%fused_computation.30.clone.1 | convolution fusion | flops 837156864 | bytes 27591684 | tf_op jit(solution)/shard_map/while/body/eval_jaxpr/while/body/eval_jaxpr/hqk,khd->qhd/dot_general | solution.py:72
  164.2 105.0 %while.67 = (s32[]{:T(128)}, bf16[2,512,12,64]{1,3,2,0:T(8,128)(2,1)}, bf16[2,512,12,64]{1,3,2,0:T(8,128)(2,1)S(1)}, bf16[1024,12,64]{0,2,1:T(8,128)(2,1)S(1)}, ...) while((s32[]{:T(128)}, bf16[2,512,12,64]{1,3,2,0:T(8,128)(2,1)}, ...), condition=%wide.region_3.4_spmd.clone, body=%wide.region_0.3_spmd.clone.sunk | while | flops 1661339648 | bytes 111724672 | solution.py:80
  175.2 30.0 %fusion.186 = (f32[12,512]{1,0:T(8,128)S(1)}, f32[12,512,1024]{2,1,0:T(8,128)}) fusion(f32[12,512,1024]{2,1,0:T(8,128)} %fusion.185, pred[1024]{0:T(1024)(128)(4,1)S(1)} %iota_compare_fusion.8), kind=kOutput, calls=%fused_computation.195.clone.1 | output fusion | flops 37749760 | bytes 50357248 | tf_op jit(solution)/shard_map/while/body/eval_jaxpr/while/body/eval_jaxpr/sub | solution.py:69
  227.3 30.1 %fusion.186 = (f32[12,512]{1,0:T(8,128)S(1)}, f32[12,512,1024]{2,1,0:T(8,128)}) fusion(f32[12,512,1024]{2,1,0:T(8,128)} %fusion.185, pred[1024]{0:T(1024)(128)(4,1)S(1)} %iota_compare_fusion.8), kind=kOutput, calls=%fused_computation.195.clone.1 | output fusion | flops 37749760 | bytes 50357248 | tf_op jit(solution)/shard_map/while/body/eval_jaxpr/while/body/eval_jaxpr/sub | solution.py:69
  257.4 11.4 %fusion.187 = bf16[2,512,12,64]{1,3,2,0:T(8,128)(2,1)} fusion(bf16[2,512,12,64]{1,3,2,0:T(8,128)(2,1)} %get-tuple-element.694, s32[]{:T(128)S(6)} %copy.112, bf16[1024,12,64]{0,2,1:T(8,128)(2,1)S(1)} %copy-done.2, f32[12,512,1024]{2,1,0:T(8,128)} %get-tuple-element.663, f32[12,512]{1,0:T(8,128)S(1)} %get-tuple-element.664), kind=kOutput, calls=%fused_computation.14.clone.1 | convolution fusion | flops 818282496 | bytes 27549700 | tf_op jit(solution)/shard_map/while/body/eval_jaxpr/while/body/eval_jaxpr/hqk,khd->qhd/dot_general | solution.py:72
  289.9 12.4 %multiply_convert_fusion.1 = (bf16[1024,3072]{1,0:T(8,128)(2,1)}, f32[1024,3072]{1,0:T(8,128)}) fusion(f32[3072]{0:T(1024)S(1)} %copy-done.52, bf16[768,3072]{1,0:T(8,128)(2,1)} %all-gather.12.cloned.1.call-done, f32[1024,768]{1,0:T(8,128)} %copy-done.5, f32[1024]{0:T(1024)S(1)} %fusion.95, f32[1024]{0:T(1024)S(1)} %broadcast_multiply_fusion.2, ...), kind=kOutput, calls=%fused_computation.68 | convolution fusion | flops 4854644736 | bytes 26765312 | tf_op jit(solution)/shard_map/dot_general | solution.py:186
  302.3 18.2 %fusion.120 = (f32[1024]{0:T(1024)S(1)}, f32[1024,768]{1,0:T(8,128)}) fusion(s32[1,1024,768]{2,1,0:T(8,128)} %param.31, f32[768]{0:T(1024)S(1)} %copy-done.57, bf16[3072,768]{1,0:T(8,128)(2,1)} %all-gather.14.cloned.1.call-done, f32[3072]{0:T(1024)S(1)} %copy-done.52, bf16[768,3072]{1,0:T(8,128)(2,1)} %all-gather.12.cloned.1.call-done, ...), kind=kOutput, calls=%fused_computation.201 | convolution fusion | flops 9694346240 | bytes 18908160 | tf_op jit(solution)/shard_map/dot_general | solution.py:190
  339.0 66.9 %all-gather.1 = f32[32,1,768]{2,1,0:T(1,128)S(1)} all-gather(f32[1,1,768]{2,1,0:T(1,128)S(1)} %reshape.392), channel_id=2, replica_groups=mesh['dp'=8,'fsdp'=4] {'dp','fsdp'}, dimensions={0}, use_global_device_ids=true | all-gather | bytes 101376 | tf_op jit(solution)/shard_map/all_gather | solution.py:281
  421.0 13.4 %convert_reduce_fusion = (f32[3072]{0:T(1024)}, bf16[1024,3072]{1,0:T(8,128)(2,1)S(1)}) fusion(bf16[1024,768]{1,0:T(8,128)(2,1)S(1)} %get-tuple-element.492, bf16[3072,768]{1,0:T(8,128)(2,1)} %all-gather.14.cloned.1.call-done, f32[1024,3072]{1,0:T(8,128)} %get-tuple-element.523, f32[3072]{0:T(1024)S(1)} %copy-done.52), kind=kOutput, calls=%fused_computation.66 | convolution fusion | flops 4882166784 | bytes 25190400 | tf_op jit(solution)/shard_map/dot_general | solution.py:340
  464.2 165.9 %while.69 = (s32[]{:T(128)}, f32[1024,12,64]{0,2,1:T(8,128)}, f32[1024,12,64]{0,2,1:T(8,128)}, bf16[2,512,12,64]{1,3,2,0:T(8,128)(2,1)}, bf16[2,512,12,64]{1,3,2...) while((s32[]{:T(128)}, f32[1024,12,64]{0,2,1:T(8,128)}, ...), condition=%wide.region_28.29_spmd.clone, body=%wide.region_26.28_spmd.clone.sunk | while | flops 4125223936 | bytes 217239728 | solution.py:128
  475.5 13.2 %bitcast_add_fusion.5 = f32[1024,12,64]{0,2,1:T(8,128)} fusion(f32[1024,12,64]{0,2,1:T(8,128)} %get-tuple-element.745, f32[12,512,1024]{2,1,0:T(8,128)} %fusion.202, f32[12,512]{1,0:T(8,128)S(1)} %dynamic-slice_bitcast_fusion.2, pred[1024]{0:T(1024)(128)(4,1)S(1)} %iota_compare_fusion.10, pred[]{:T(512)S(6)} %compare.9, ...), kind=kOutput, calls=%fused_computation.45.clone.1 | convolution fusion | flops 832045056 | bytes 32277508 | tf_op jit(solution)/shard_map/while/body/eval_jaxpr/while/body/eval_jaxpr/hqk,qhd->khd/dot_general | solution.py:108
  488.6 17.9 %multiply_reduce_fusion.13 = (f32[12,512]{1,0:T(8,128)S(1)}, f32[12,512,1024]{2,1,0:T(8,128)}) fusion(f32[12,512,1024]{2,1,0:T(8,128)} %fusion.202, f32[12,512]{1,0:T(8,128)S(1)} %dynamic-slice_bitcast_fusion.2, pred[1024]{0:T(1024)(128)(4,1)S(1)} %iota_compare_fusion.10, bf16[1024,12,64]{0,2,1:T(8,128)(2,1)} %get-tuple-element.763, ...), kind=kOutput, calls=%fused_computation.40.clone.1 | convolution fusion | flops 836757504 | bytes 52741124 | tf_op jit(solution)/shard_map/while/body/eval_jaxpr/while/body/eval_jaxpr/qhd,khd->hqk/dot_general | solution.py:103
  506.5 21.7 %multiply_convert_fusion.7 = bf16[12,512,1024]{2,1,0:T(8,128)(2,1)} fusion(f32[12,512,1024]{2,1,0:T(8,128)} %get-tuple-element.684, f32[12,512,1024]{2,1,0:T(8,128)} %fusion.202, f32[12,512]{1,0:T(8,128)S(1)} %get-tuple-element.685, f32[12,512]{1,0:T(8,128)S(1)} %dynamic-slice_bitcast_fusion.2, pred[1024]{0:T(1024)(128)(4,1)S(1)} %iota_compare_fusion.10), kind=kLoop, calls=%fused_computation.39.clone.1 | loop fusion | flops 37748736 | bytes 62964736 | tf_op jit(solution)/shard_map/while/body/eval_jaxpr/while/body/eval_jaxpr/convert_element_type | solution.py:107
  557.2 14.1 %bitcast_add_fusion.5 = f32[1024,12,64]{0,2,1:T(8,128)} fusion(f32[1024,12,64]{0,2,1:T(8,128)} %get-tuple-element.745, f32[12,512,1024]{2,1,0:T(8,128)} %fusion.202, f32[12,512]{1,0:T(8,128)S(1)} %dynamic-slice_bitcast_fusion.2, pred[1024]{0:T(1024)(128)(4,1)S(1)} %iota_compare_fusion.10, pred[]{:T(512)S(6)} %compare.9, ...), kind=kOutput, calls=%fused_computation.45.clone.1 | convolution fusion | flops 832045056 | bytes 32277508 | tf_op jit(solution)/shard_map/while/body/eval_jaxpr/while/body/eval_jaxpr/hqk,qhd->khd/dot_general | solution.py:108
  571.4 17.7 %multiply_reduce_fusion.13 = (f32[12,512]{1,0:T(8,128)S(1)}, f32[12,512,1024]{2,1,0:T(8,128)}) fusion(f32[12,512,1024]{2,1,0:T(8,128)} %fusion.202, f32[12,512]{1,0:T(8,128)S(1)} %dynamic-slice_bitcast_fusion.2, pred[1024]{0:T(1024)(128)(4,1)S(1)} %iota_compare_fusion.10, bf16[1024,12,64]{0,2,1:T(8,128)(2,1)} %get-tuple-element.763, ...), kind=kOutput, calls=%fused_computation.40.clone.1 | convolution fusion | flops 836757504 | bytes 52741124 | tf_op jit(solution)/shard_map/while/body/eval_jaxpr/while/body/eval_jaxpr/qhd,khd->hqk/dot_general | solution.py:103
  589.1 22.0 %multiply_convert_fusion.7 = bf16[12,512,1024]{2,1,0:T(8,128)(2,1)} fusion(f32[12,512,1024]{2,1,0:T(8,128)} %get-tuple-element.684, f32[12,512,1024]{2,1,0:T(8,128)} %fusion.202, f32[12,512]{1,0:T(8,128)S(1)} %get-tuple-element.685, f32[12,512]{1,0:T(8,128)S(1)} %dynamic-slice_bitcast_fusion.2, pred[1024]{0:T(1024)(128)(4,1)S(1)} %iota_compare_fusion.10), kind=kLoop, calls=%fused_computation.39.clone.1 | loop fusion | flops 37748736 | bytes 62964736 | tf_op jit(solution)/shard_map/while/body/eval_jaxpr/while/body/eval_jaxpr/convert_element_type | solution.py:107
  683.4 38.7 %all-reduce.18 = (f32[1536]{0:T(1024)S(1)}, f32[768]{0:T(1024)S(1)}, f32[768]{0:T(1024)S(1)}, f32[768]{0:T(1024)S(1)}, f32[3072]{0:T(1024)S(1)}, /*index=5*/f32[...) all-reduce(f32[1536]{0:T(1024)S(1)} %pad_maximum_fusion.1, ...), channel_id=4, replica_groups=mesh['dp'=8,'fsdp'=4] {'dp','fsdp'}, use_global_device_ids=true, to_apply=%region_31.32.clone | all-reduce | flops 9984 | bytes 78336
  737.3 35.3 %reduce-scatter.16.cloned.1.call-done = f32[24,2304]{1,0:T(8,128)} async-done(((f32[768,2304]{1,0:T(8,128)}), f32[24,2304]{1,0:T(8,128)}) %reduce-scatter.16.cloned.1.call-update) | async-done | bytes 221200
  772.6 142.3 %reduce-scatter.10.cloned.1.call-done = f32[24,3072]{1,0:T(8,128)} async-done(((f32[768,3072]{1,0:T(8,128)}), f32[24,3072]{1,0:T(8,128)}) %reduce-scatter.10.cloned.1.call-update) | async-done | bytes 294928 | tf_op jit(solution)/shard_map/reduce_scatter | solution.py:396
  914.9 140.9 %reduce-scatter.12.cloned.1.call-done = f32[96,768]{1,0:T(8,128)} async-done(((f32[3072,768]{1,0:T(8,128)}), f32[96,768]{1,0:T(8,128)}) %reduce-scatter.12.cloned.1.call-update) | async-done | bytes 294928 | tf_op jit(solution)/shard_map/reduce_scatter | solution.py:398
  (322 shorter events, 322.4 us)
Async XLA Ops:
  7.2 66.8 %all-gather.8.cloned.1.call-start = ((), (), s32[]{:S(2)}) async-start(), calls=%async_computation.5 | async-start | bytes 3649536 | tf_op jit(solution)/shard_map/all_gather | solution.py:262
  7.9 269.2 %all-gather.10.cloned.1.call-start = ((), (), s32[]{:S(2)}) async-start(), calls=%async_computation.6 | async-start | bytes 1216512 | tf_op jit(solution)/shard_map/all_gather | solution.py:264
  8.7 281.2 %all-gather.12.cloned.1.call-start = ((), (), s32[]{:S(2)}) async-start(), calls=%async_computation.7 | async-start | bytes 4866048 | tf_op jit(solution)/shard_map/all_gather | solution.py:268
  9.4 292.9 %all-gather.14.cloned.1.call-start = ((), (), s32[]{:S(2)}) async-start(), calls=%async_computation.8 | async-start | bytes 4866048 | tf_op jit(solution)/shard_map/all_gather | solution.py:270
  10.0 325.8 %all-gather.16.cloned.1.call-start = ((), (), s32[]{:S(2)}) async-start(), calls=%async_computation.9 | async-start | bytes 1216512 | tf_op jit(solution)/shard_map/all_gather | solution.py:274
  10.6 726.7 %reduce-scatter.8.cloned.1.call-start = ((), (), s32[]{:S(2)}) async-start(), calls=%async_computation.10 | async-start | bytes 2433024 | tf_op jit(solution)/shard_map/reduce_scatter | solution.py:392
  175.2 30.0 %copy-start.2 = (bf16[1024,12,64]{0,2,1:T(8,128)(2,1)S(1)}, bf16[1024,12,64]{0,2,1:T(8,128)(2,1)}, u32[]{:S(2)}) copy-start(bf16[1024,12,64]{0,2,1:T(8,128)(2,1)} %get-tuple-element.704) | copy-start | bytes 4718596 | tf_op jit(solution)/shard_map/while/body/eval_jaxpr/while
  227.3 30.1 %copy-start.2 = (bf16[1024,12,64]{0,2,1:T(8,128)(2,1)S(1)}, bf16[1024,12,64]{0,2,1:T(8,128)(2,1)}, u32[]{:S(2)}) copy-start(bf16[1024,12,64]{0,2,1:T(8,128)(2,1)} %get-tuple-element.704) | copy-start | bytes 4718596 | tf_op jit(solution)/shard_map/while/body/eval_jaxpr/while
  287.6 153.2 %copy-start.32 = (f32[1024]{0:T(1024)}, f32[1024]{0:T(1024)S(1)}, u32[]{:S(2)}) copy-start(f32[1024]{0:T(1024)S(1)} %broadcast_multiply_fusion.2) | copy-start | bytes 12292
  289.8 151.0 %copy-start.34 = (f32[1024]{0:T(1024)}, f32[1024]{0:T(1024)S(1)}, u32[]{:S(2)}) copy-start(f32[1024]{0:T(1024)S(1)} %fusion.95) | copy-start | bytes 12292
  334.0 73.0 %copy-start.54 = (s32[32]{0:T(128)S(1)}, s32[32]{0:T(128)}, u32[]{:S(2)}) copy-start(s32[32]{0:T(128)} %param.32) | copy-start | bytes 388
  335.7 74.6 %copy-start.13 = (bf16[768,768]{1,0:T(8,128)(2,1)S(1)}, bf16[768,768]{1,0:T(8,128)(2,1)}, u32[]{:S(2)}) copy-start(bf16[768,768]{1,0:T(8,128)(2,1)} %all-gather.16.cloned.1.call-done) | copy-start | bytes 3538948
  410.3 38.5 %copy-start.44 = (bf16[768]{0:T(1024)(128)(2,1)}, bf16[768]{0:T(1024)(128)(2,1)S(1)}, u32[]{:S(2)}) copy-start(bf16[768]{0:T(1024)(128)(2,1)S(1)} %get-tuple-element.489) | copy-start | bytes 4612
  419.8 14.6 %slice-start = ((s8[4718592]{0:T(1024)(128)(4,1)}), s8[4194304]{0:T(1024)(128)(4,1)S(1)}, s32[]{:S(2)}) async-start(s8[4718592]{0:T(1024)(128)(4,1)} %bitcast.241), calls=%async_computation.15 | async-start | bytes 8388608
  421.0 13.4 %slice-start.1 = ((s8[4718592]{0:T(1024)(128)(4,1)}), s8[524288]{0:T(1024)(128)(4,1)S(1)}, s32[]{:S(2)}) async-start(s8[4718592]{0:T(1024)(128)(4,1)} %bitcast.241), calls=%async_computation.16 | async-start | bytes 1048576
  448.0 289.3 %reduce-scatter.14.cloned.1.call-start = ((), (), s32[]{:S(2)}) async-start(), calls=%async_computation.13 | async-start | bytes 2433024 | tf_op jit(solution)/shard_map/reduce_scatter | solution.py:402
  464.2 308.5 %reduce-scatter.16.cloned.1.call-start = ((), (), s32[]{:S(2)}) async-start(), calls=%async_computation.14 | async-start | bytes 7299072
  655.5 259.4 %reduce-scatter.10.cloned.1.call-start = ((), (), s32[]{:S(2)}) async-start(), calls=%async_computation.11 | async-start | bytes 9732096 | tf_op jit(solution)/shard_map/reduce_scatter | solution.py:396
  668.3 387.6 %reduce-scatter.12.cloned.1.call-start = ((), (), s32[]{:S(2)}) async-start(), calls=%async_computation.12 | async-start | bytes 9732096 | tf_op jit(solution)/shard_map/reduce_scatter | solution.py:398
  680.2 46.0 %copy-start.43 = (f32[32]{0:T(128)S(1)}, f32[32]{0:T(128)}, u32[]{:S(2)}) copy-start(f32[32]{0:T(128)} %copy-done.42) | copy-start | bytes 388
  680.2 46.0 %copy-start.61 = (f32[32]{0:T(128)S(1)}, f32[32]{0:T(128)}, u32[]{:S(2)}) copy-start(f32[32]{0:T(128)} %copy-done.60) | copy-start | bytes 388
  680.2 46.0 %copy-start.62 = (f32[32]{0:T(128)S(1)}, f32[32]{0:T(128)}, u32[]{:S(2)}) copy-start(f32[32]{0:T(128)} %get-tuple-element.424) | copy-start | bytes 388
  680.2 48.4 %copy-start.12 = (f32[1024,768]{1,0:T(8,128)S(1)}, f32[1024,768]{1,0:T(8,128)}, u32[]{:S(2)}) copy-start(f32[1024,768]{1,0:T(8,128)} %copy-done.11) | copy-start | bytes 9437188
  680.2 48.4 %copy-start.51 = (f32[1024]{0:T(1024)S(1)}, f32[1024]{0:T(1024)}, u32[]{:S(2)}) copy-start(f32[1024]{0:T(1024)} %copy-done.50) | copy-start | bytes 12292
  (60 other events, 266.4 us)
Sparse Core Ops, SparseCore 0:
  10.9 63.0 all-gather.7
  76.9 52.8 all-gather.9
  132.7 62.5 all-gather.11
  198.1 62.3 all-gather.13
  263.2 52.8 all-gather.15
  448.1 94.8 reduce-scatter.7
  549.7 97.9 reduce-scatter.13
  655.7 116.9 reduce-scatter.15
  780.1 134.7 reduce-scatter.9
  921.2 134.5 reduce-scatter.11
where the time goes:
time: 1070 us; the launch traced here: 1060 us
  matrix products  332 us (31%)
  waiting for transfers between devices  326 us (30%)
  other arithmetic  166 us (16%)
  blocking collectives  149 us (14%)
  local copies, waits for them, and re-layouts  72.7 us (7%)
  between operations  17.4 us (2%)
    reduce_scatter x1, waiting for transfers between devices, on_device(): lax.psum_scatter(up_weight_grad, ('dp', 'fsdp'), scatter_dimension=0, til...  142 us
    reduce_scatter x1, waiting for transfers between devices, on_device(): lax.psum_scatter(down_weight_grad, ('dp', 'fsdp'), scatter_dimension=0, t...  141 us
    unnamed x2, blocking collectives  81.6 us
    all_gather x1, blocking collectives, on_device(): lax.all_gather(forward_state['pooled'], ('dp', 'fsdp'), axis=0, tiled=True)  66.9 us
    dot_general x6, matrix products, block_scores(): jnp.einsum('qhd,khd->hqk', query_block, key_rows, preferred_element_type=...  61.2 us
    sub x2, other arithmetic, per_block(): shifted = jnp.exp(scores - row_max)  60.1 us
    dot_general x4, matrix products, per_block(): jnp.einsum('hqk,khd->qhd', probabilities, sequence_value_rows, preferred_...  45.1 us
    convert_element_type x2, other arithmetic, per_block(): score_grad = (probabilities * (prob_grad - inner_sum)).astype(jnp.bfloat16)  43.7 us
  transfers between devices with their start and end apart: 10, of which 4 were waited for; matrix products, arithmetic and copies ran while one was open for 48% of the time, Pallas kernels for 0%

commit v1 on v0

v1 whole, which is shorter than its diff:
```python
import functools
import math

import jax
import jax.numpy as jnp
from jax import lax
from jax.experimental import pallas as pl
from jax.experimental.pallas import tpu as pltpu
from jax.sharding import PartitionSpec as P

HEAD_DIM = 64
LANES = 128
f32, bf16 = jnp.float32, jnp.bfloat16
MESH = pl.DeviceIdType.MESH
AXES = ("dp", "fsdp")
eps_norm = 1e-05
keep_scale = 1.0 / 0.9
logit_divisor = 0.05
neg_fill = -1000000000.0
VMEM_LIMIT = 67043328
DIMS = ("z", "c", "y", "x")
GATHER_ORDERS = (("z", "x", "y", "c"), ("z", "y", "x", "c"))
SCATTER_ORDERS = (("c", "y", "x", "z"), ("c", "x", "y", "z"))
LAG = 2


class Grid:
    def __init__(self, mesh, with_fsdp=True):
        dp, fsdp = mesh.shape["dp"], mesh.shape["fsdp"]
        cores = 2 if dp % 2 == 0 else 1
        side = math.isqrt(fsdp)
        if side * side != fsdp:
            side = fsdp
        self.with_fsdp = with_fsdp
        self.size = {
            "z": dp // cores,
            "c": cores,
            "y": fsdp // side if with_fsdp else 1,
            "x": side if with_fsdp else 1,
        }
        self.shape = tuple(self.size[d] for d in DIMS)
        self.count = math.prod(self.shape)
        self.slots = sum(n - 1 for n in self.shape)

    def me(self):
        dp, fsdp = lax.axis_index("dp"), lax.axis_index("fsdp")
        at = {"z": lax.div(dp, self.size["c"]), "c": lax.rem(dp, self.size["c"])}
        if self.with_fsdp:
            at["y"], at["x"] = lax.div(fsdp, self.size["x"]), lax.rem(fsdp, self.size["x"])
        else:
            at["y"], at["x"] = 0, 0
        return at

    def device(self, at):
        fsdp = at["y"] * self.size["x"] + at["x"] if self.with_fsdp else lax.axis_index("fsdp")
        return (at["z"] * self.size["c"] + at["c"], fsdp)

    def peer(self, at, dim, j):
        other = dict(at)
        other[dim] = lax.rem(at[dim] + j, self.size[dim])
        return other

    def slot(self, dim, j):
        base = 0
        for d in DIMS:
            if d == dim:
                return base + j - 1
            base += self.size[d] - 1

    def order(self, order):
        return tuple(d for d in order if self.size[d] > 1)

    def barrier(self):
        at, sem, count = self.me(), pltpu.get_barrier_semaphore(), 0
        for d in DIMS:
            for j in range(1, self.size[d]):
                pl.semaphore_signal(
                    sem, inc=1, device_id=self.device(self.peer(at, d, j)), device_id_type=MESH
                )
                count += 1
        pl.semaphore_wait(sem, count)


class Gather:
    def __init__(self, grid, pieces, send, recv):
        self.grid, self.send, self.recv, self.at = grid, send, recv, grid.me()
        self.pieces = [(ref, sub, grid.order(order)) for ref, sub, order in pieces]
        self.stages = len(self.pieces[0][2])
        self.steps = len(pieces) + (self.stages - 1) * LAG
        self.now = 0

    def copies(self, i, stage):
        ref, sub, order = self.pieces[i]
        dim, done = order[stage], order[:stage]
        index = tuple(slice(None) if d in done else self.at[d] for d in DIMS)
        view = ref.at[index + sub]
        for j in range(1, self.grid.size[dim]):
            slot = self.grid.slot(dim, j)
            yield pltpu.make_async_remote_copy(
                src_ref=view,
                dst_ref=view,
                send_sem=self.send.at[i, slot],
                recv_sem=self.recv.at[i, slot],
                device_id=self.grid.device(self.grid.peer(self.at, dim, j)),
                device_id_type=MESH,
            )

    def begin(self):
        for i in range(len(self.pieces)):
            for copy in self.copies(i, 0):
                copy.start()

    def run(self, first, last):
        for step in range(first, last):
            for stage in range(self.stages):
                i = step - stage * LAG
                if 0 <= i < len(self.pieces):
                    for copy in self.copies(i, stage):
                        copy.wait_recv()
                    if stage < self.stages - 1:
                        for copy in self.copies(i, stage + 1):
                            copy.start()

    def until(self, i):
        last = max(self.now, min(self.steps, i + 1 + (self.stages - 1) * LAG))
        self.run(self.now, last)
        self.now = last

    def finish(self):
        self.run(self.now, self.steps)
        for i in range(len(self.pieces)):
            for stage in range(self.stages):
                for copy in self.copies(i, stage):
                    copy.wait_send()


class Scatter:
    def __init__(self, grid, pieces, send, recv):
        self.grid, self.send, self.recv, self.at = grid, send, recv, grid.me()
        self.pieces = [(src, sub, grid.order(order), bufs, out) for src, sub, order, bufs, out in pieces]
        self.stages = len(self.pieces[0][2])
        self.steps = len(pieces) + (self.stages - 1) * LAG

    def pick(self, i, stage, where):
        src, sub, order, bufs, _ = self.pieces[i]
        left = tuple(d for d in DIMS if d not in order[:stage])
        index = tuple(where if d == order[stage] else slice(None) for d in left)
        if stage == 0:
            return src.at[index + sub]
        return bufs[stage - 1].at[(0,) + index]

    def copies(self, i, stage):
        _, _, order, bufs, _ = self.pieces[i]
        dim = order[stage]
        for j in range(1, self.grid.size[dim]):
            other = self.grid.peer(self.at, dim, j)
            slot = self.grid.slot(dim, j)
            yield pltpu.make_async_remote_copy(
                src_ref=self.pick(i, stage, other[dim]),
                dst_ref=bufs[stage].at[j - 1],
                send_sem=self.send.at[i, slot],
                recv_sem=self.recv.at[i, slot],
                device_id=self.grid.device(other),
                device_id_type=MESH,
            )

    def begin(self, i):
        for copy in self.copies(i, 0):
            copy.start()

    def run(self, first, last):
        for step in range(first, last):
            for stage in range(self.stages):
                i = step - stage * LAG
                if 0 <= i < len(self.pieces):
                    self.add(i, stage)
                    if stage < self.stages - 1:
                        for copy in self.copies(i, stage + 1):
                            copy.start()

    def add(self, i, stage):
        _, _, order, bufs, out = self.pieces[i]
        for copy in self.copies(i, stage):
            copy.wait_recv()
        buf = bufs[stage]
        total = self.pick(i, stage, self.at[order[stage]])[...].astype(f32)
        for j in range(self.grid.size[order[stage]] - 1):
            total = total + buf[j].astype(f32)
        if stage == self.stages - 1:
            out[...] = total.reshape(out.shape)
        else:
            buf[0] = total.astype(buf.dtype)

    def finish(self):
        for i in range(len(self.pieces)):
            for stage in range(self.stages):
                for copy in self.copies(i, stage):
                    copy.wait_send()


def scatter_buffers(grid, order, rows, columns, dtype):
    shapes, left = [], list(DIMS)
    for d in grid.order(order):
        left.remove(d)
        shapes.append((grid.size[d] - 1,) + tuple(grid.size[e] for e in left) + (rows, columns))
    return [pltpu.VMEM(s, dtype) for s in shapes]


def cuts(total, parts, unit):
    while parts > 1 and total % (parts * unit):
        parts -= 1
    return [(j * (total // parts), total // parts) for j in range(parts)]


def dotg(a, b, ca, cb, precision=None):
    return lax.dot_general(
        a, b, (((ca,), (cb,)), ((), ())), preferred_element_type=f32, precision=precision
    )


def iota(shape, dim):
    return lax.broadcasted_iota(jnp.int32, shape, dim)


def three_parts(x):
    high = x.astype(bf16).astype(f32)
    mid = (x - high).astype(bf16).astype(f32)
    return high, mid, x - high - mid


def spread_vector(rows, n):
    shards, width = rows.shape
    total = shards * n
    place = (iota((width, total), 1) % n == iota((width, total), 0)).astype(f32).astype(bf16)
    wide = dotg(rows, place, 1, 0)
    keep = iota((shards, total), 1) // n == iota((shards, total), 0)
    return jnp.sum(jnp.where(keep, wide, 0.0), axis=0, keepdims=True)


def fold_vector(vector, shards, n, width):
    total = shards * n
    keep = iota((shards, total), 1) // n == iota((shards, total), 0)
    place = (iota((total, width), 0) % n == iota((total, width), 1)).astype(f32)
    return dotg(jnp.where(keep, vector, 0.0), place, 1, 0, lax.Precision.HIGHEST)


def attend(qkv_ref, context_ref, lse_ref, live, pair, block, tick):
    length, width = qkv_ref.shape[0], context_ref.shape[1]

    def col(part):
        return pl.ds(pl.multiple_of(part * width + pair * LANES, LANES), LANES)

    k = qkv_ref[:, col(1)].astype(f32) * (1.0 / math.sqrt(HEAD_DIM))
    v = qkv_ref[:, col(2)].astype(f32)
    lane, row = iota((length, LANES), 1), iota((length, LANES), 0)
    bias = jnp.where(row < live, 0.0, neg_fill)
    keys, values = [], []
    for h in range(2):
        mine, spare = lane // HEAD_DIM == h, HEAD_DIM * (1 - h)
        keys.append(jnp.where(mine, k, jnp.where(lane == spare, bias, 0.0)).astype(bf16))
        values.append(jnp.where(mine, v, 1.0).astype(bf16))
    lane = iota((block, LANES), 1)
    low = lane < HEAD_DIM
    for i in range(length // block):
        rows = slice(i * block, (i + 1) * block)
        q = qkv_ref[rows, col(0)].astype(f32)
        sums, tops = [], []
        for h in range(2):
            spare = HEAD_DIM * (1 - h)
            qh = jnp.where(lane // HEAD_DIM == h, q, jnp.where(lane == spare, 1.0, 0.0))
            scores = dotg(qh.astype(bf16), keys[h], 1, 1)
            top = jnp.max(scores, axis=1, keepdims=True)
            weights = jnp.exp(scores - top).astype(bf16)
            sums.append(dotg(weights, values[h], 1, 0))
            tops.append(top)
        num = jnp.where(low, sums[0], sums[1])
        den = pltpu.roll(jnp.where(low, sums[1], sums[0]), HEAD_DIM, 1)
        out = pl.ds(pl.multiple_of(pair * LANES, LANES), LANES)
        context_ref[rows, out] = (num / den).astype(bf16)
        lse_ref[rows, out] = jnp.where(low, tops[0], tops[1]) + jnp.log(den)
        tick(i)


def gather_plan(grid, shapes):
    plan = [("s", ())]
    every = slice(None)
    for name, parts in (("q", 6), ("o", 2), ("u", 6), ("d", 6), ("p", 2)):
        rows, columns = shapes[name]
        if name == "d":
            plan += [(name, (pl.ds(a, n), every)) for a, n in cuts(rows, parts, 8)]
        else:
            plan += [(name, (every, pl.ds(a, n))) for a, n in cuts(columns, parts, LANES)]
    return [(name, sub, GATHER_ORDERS[i % 2]) for i, (name, sub) in enumerate(plan)]


def forward_kernel(grid, plan, sizes, len_ref, tokens_ref, wq, wo, wu, wd, wp, *refs):
    count = len(sizes)
    small_in, refs = refs[:count], refs[count:]
    (gq, go, gu, gd, gp, qkv_ref, context_ref, lse_ref), refs = refs[:8], refs[8:]
    small_out, (gs, send, recv, own_sem) = refs[:count], refs[count:]
    at = grid.me()
    own = tuple(at[d] for d in DIMS)
    to_own = []
    for i, (src, dst) in enumerate(((wq, gq), (wo, go), (wu, gu), (wd, gd), (wp, gp))):
        to_own.append(pltpu.make_async_copy(src, dst.at[own], own_sem.at[i]))
        to_own[-1].start()
    mine = gs.at[own]
    mine[...] = jnp.zeros(mine.shape, bf16)
    for i, (ref, n) in enumerate(zip(small_in, sizes)):
        mine[i : i + 1, 0:n] = ref[...]
    where = dict(q=gq, o=go, u=gu, d=gd, p=gp, s=gs)
    gather = Gather(grid, [(where[name], sub, order) for name, sub, order in plan], send, recv)
    grid.barrier()
    for copy in to_own:
        copy.wait()
    gather.begin()
    gather.until(0)
    rows = gs[...].reshape((grid.count,) + gs.shape[-2:])
    for i, (ref, n) in enumerate(zip(small_out, sizes)):
        ref[...] = spread_vector(rows[:, i, :], n)
    width = context_ref.shape[1]
    tokens = tokens_ref[...]
    for i, (name, sub, _) in enumerate(plan):
        if name != "q":
            continue
        gather.until(i)
        lo, n = sub[1].start, sub[1].size

        def project(weight, sem):
            copy = pltpu.make_async_copy(gq.at[:, :, :, :, :, pl.ds(lo, n)], weight, sem)
            copy.start()
            copy.wait()
            out = dotg(tokens, weight[...].reshape(-1, n), 1, 0)
            if lo < width:
                out = out + small_out[0][:, lo : lo + n]
            elif lo >= 2 * width:
                out = out + small_out[0][:, lo - width : lo - width + n]
            qkv_ref[:, lo : lo + n] = out.astype(bf16)

        pl.run_scoped(project, pltpu.VMEM(gq.shape[:-1] + (n,), bf16), pltpu.SemaphoreType.DMA)
    pairs, block = width // LANES, min(512, qkv_ref.shape[0])
    blocks = qkv_ref.shape[0] // block
    first, todo, slots = gather.now, gather.steps - gather.now, pairs * blocks
    live = len_ref[0]

    def one_pair(pair, _):
        def tick(i):
            for p in range(pairs):
                t = p * blocks + i

                @pl.when(pair == p)
                def _():
                    gather.run(first + t * todo // slots, first + (t + 1) * todo // slots)

        attend(qkv_ref, context_ref, lse_ref, live, pair, block, tick)
        return 0

    lax.fori_loop(0, pairs, one_pair, 0)
    gather.now = gather.steps
    gather.finish()


def run_forward(grid, length_of, tokens, big, small):
    length, width = tokens.shape
    names = ("q", "o", "u", "d", "p")
    shapes = {k: w.shape for k, w in zip(names, big)}
    sizes = [v.shape[0] for v in small]
    plan = gather_plan(grid, shapes)
    pad = -(-max(sizes) // LANES) * LANES
    vmem, anywhere = pl.BlockSpec(memory_space=pltpu.VMEM), pl.BlockSpec(memory_space=pl.ANY)
    outs = pl.pallas_call(
        functools.partial(forward_kernel, grid, plan, sizes),
        out_shape=[jax.ShapeDtypeStruct(grid.shape + shapes[k], bf16) for k in names]
        + [
            jax.ShapeDtypeStruct((length, 3 * width), bf16),
            jax.ShapeDtypeStruct((length, width), bf16),
            jax.ShapeDtypeStruct((length, width), f32),
        ]
        + [jax.ShapeDtypeStruct((1, grid.count * n), f32) for n in sizes],
        in_specs=[pl.BlockSpec(memory_space=pltpu.SMEM)] + [vmem] * (6 + len(small)),
        out_specs=[anywhere] * 5 + [vmem] * (3 + len(small)),
        scratch_shapes=[
            pltpu.VMEM(grid.shape + (16, pad), bf16),
            pltpu.SemaphoreType.DMA((len(plan), grid.slots)),
            pltpu.SemaphoreType.DMA((len(plan), grid.slots)),
            pltpu.SemaphoreType.DMA((5,)),
        ],
        compiler_params=pltpu.CompilerParams(
            collective_id=0, has_side_effects=True, vmem_limit_bytes=VMEM_LIMIT
        ),
        name="gather_and_attend",
    )(length_of, tokens, *big, *[v.reshape(1, -1) for v in small])
    gathered = [g.reshape(-1, g.shape[-1]) for g in outs[:5]]
    return gathered, outs[5], outs[6], outs[7], outs[8:]


def exchange_kernel(grid, row_ref, all_ref, send, recv):
    at = grid.me()
    all_ref[tuple(at[d] for d in DIMS)] = row_ref[...]
    gather = Gather(grid, [(all_ref, (), GATHER_ORDERS[0])], send, recv)
    grid.barrier()
    gather.begin()
    gather.finish()


def exchange(grid, rows):
    vmem = pl.BlockSpec(memory_space=pltpu.VMEM)
    out = pl.pallas_call(
        functools.partial(exchange_kernel, grid),
        out_shape=jax.ShapeDtypeStruct(grid.shape + rows.shape, rows.dtype),
        in_specs=[vmem],
        out_specs=vmem,
        scratch_shapes=[pltpu.SemaphoreType.DMA((1, grid.slots))] * 2,
        compiler_params=pltpu.CompilerParams(collective_id=1, has_side_effects=True),
        name="exchange",
    )(rows)
    return out.reshape((-1,) + rows.shape)


def attend_back(qkv_ref, context, dcontext, lse, live, pair, block, prep, acc, tick):
    length, width = qkv_ref.shape[0], context.shape[1]
    scale = 1.0 / math.sqrt(HEAD_DIM)
    one = pl.ds(pl.multiple_of(pair * LANES, LANES), LANES)

    def col(part):
        return pl.ds(pl.multiple_of(part * width + pair * LANES, LANES), LANES)

    q, k, v = (qkv_ref[:, col(j)].astype(f32) for j in range(3))
    d = dcontext[:, one].astype(f32)
    lane, row = iota((length, LANES), 1), iota((length, LANES), 0)
    bias = jnp.where(row < live, 0.0, neg_fill)
    both = d * context[:, one].astype(f32)
    total = lse[:, one]
    other = pltpu.roll(total, HEAD_DIM, 1)
    for h in range(2):
        mine, a = lane // HEAD_DIM == h, HEAD_DIM * (1 - h)
        inner = jnp.sum(jnp.where(mine, both, 0.0), axis=1, keepdims=True)
        l0, l1, l2 = three_parts(-other)
        d0, d1, d2 = three_parts(-inner)

        def lanes(base, *extra):
            out = 0.0
            for j, e in reversed(list(enumerate(extra))):
                out = jnp.where(lane == a + j, e, out)
            return jnp.where(mine, base, out).astype(bf16)

        prep[h, 0] = lanes(q * scale, 1.0, l0, l1, l2)
        prep[h, 1] = lanes(k, bias, 1.0, 1.0, 1.0)
        prep[h, 2] = lanes(d, d0, d1, d2)
        prep[h, 3] = lanes(v, 1.0, 1.0, 1.0)
        prep[h, 4] = lanes(q * scale)
        prep[h, 5] = lanes(d)
        prep[h, 6] = lanes(k * scale)
    q_t = (q * scale).T.astype(bf16)
    d_t = d.T.astype(bf16)
    acc[...] = jnp.zeros_like(acc)
    for i in range(length // block):
        rows = slice(i * block, (i + 1) * block)
        dq = jnp.zeros((block, LANES), f32)
        for h in range(2):
            head = slice(h * HEAD_DIM, (h + 1) * HEAD_DIM)
            p = jnp.exp(dotg(prep[h, 0, rows, :], prep[h, 1], 1, 1))
            dp = dotg(prep[h, 2, rows, :], prep[h, 3], 1, 1)
            ds = (p * dp).astype(bf16)
            acc[0, head, :] += dotg(d_t[head, rows], p.astype(bf16), 1, 0)
            acc[1, head, :] += dotg(q_t[head, rows], ds, 1, 0)
            dq = dq + dotg(ds, prep[h, 6], 1, 0)
        qkv_ref[rows, col(0)] = dq.astype(bf16)
        tick(i)
    qkv_ref[:, col(1)] = acc[1].T.astype(bf16)
    qkv_ref[:, col(2)] = acc[0].T.astype(bf16)


def scatter_plan(grid, shapes):
    plan, every = [], slice(None)
    for name, parts in (("d", 6), ("u", 6), ("o", 2), ("q", 9)):
        rows, columns = shapes[name]
        if name == "d":
            plan += [(name, (pl.ds(a, n), every), n, columns) for a, n in cuts(rows, parts, 8)]
        else:
            plan += [(name, (every, pl.ds(a, n)), rows, n) for a, n in cuts(columns, parts, LANES)]
    plan.append(("s", (), 16, shapes["s"]))
    return [(p[0], p[1], SCATTER_ORDERS[i % 2]) + p[2:] for i, p in enumerate(plan)]


def backward_kernel(grid, plan, sizes, len_ref, qkv_hbm, context, dcontext, lse, tokens, first_grad, wq, dd, du, do, *refs):
    count = len(sizes)
    small_in, refs = refs[: count - 1], refs[count - 1 :]
    (rq, ro, ru, rd, rs, tokens_grad), refs = refs[:6], refs[6:]
    (qkv_ref, dq, dsmall, prep, acc, send, recv, sem), bufs = refs[:8], list(refs[8:])
    load = pltpu.make_async_copy(qkv_hbm, qkv_ref, sem)
    load.start()
    sources, results = dict(d=dd, u=du, o=do, q=dq, s=dsmall), dict(d=rd, u=ru, o=ro, q=rq, s=rs)
    pieces = []
    for name, sub, order, _, _ in plan:
        n = len(grid.order(order))
        pieces.append((sources[name], sub, order, bufs[:n], results[name].at[sub] if sub else results[name]))
        bufs = bufs[n:]
    scatter = Scatter(grid, pieces, send, recv)
    names = [p[0] for p in plan]
    ready = names.index("q")
    grid.barrier()
    for i in range(ready):
        scatter.begin(i)
    load.wait()
    length, width = context.shape
    pairs, block = width // LANES, min(256, length)
    blocks = length // block
    slots, live = pairs * blocks, len_ref[0]

    def one_pair(pair, _):
        def tick(i):
            for p in range(pairs):
                t = p * blocks + i

                @pl.when(pair == p)
                def _():
                    scatter.run(t * ready // slots, (t + 1) * ready // slots)

        attend_back(qkv_ref, context, dcontext, lse, live, pair, block, prep, acc, tick)
        return 0

    lax.fori_loop(0, pairs, one_pair, 0)
    step = ready
    for i in range(ready, len(plan) - 1):
        sub = plan[i][1]
        part = dotg(tokens[...], qkv_ref[:, sub[1].start : sub[1].start + sub[1].size], 0, 0)
        dq[:, :, :, :, :, sub[1]] = part.astype(bf16).reshape(grid.shape + (-1, sub[1].size))
        scatter.begin(i)
        if i - 2 >= ready:
            scatter.run(step, step + 1)
            step += 1
    sums = dotg(jnp.ones((8, length), bf16), qkv_ref[...], 1, 0)[0:1]
    vectors = [jnp.concatenate([sums[:, :width], sums[:, 2 * width :]], axis=1)] + [r[...] for r in small_in]
    pad = dsmall.shape[-1]
    dsmall[...] = jnp.zeros_like(dsmall)
    for j, (v, n) in enumerate(zip(vectors, sizes)):
        dsmall[:, :, :, :, j, :] = fold_vector(v, grid.count, n, pad).reshape(grid.shape + (pad,))
    scatter.begin(len(plan) - 1)
    rest = scatter.steps - step
    parts = 4
    rows = length // parts
    for i in range(parts):
        scatter.run(step + i * rest // parts, step + (i + 1) * rest // parts)
        here = slice(i * rows, (i + 1) * rows)
        grad = first_grad[here, :] + dotg(qkv_ref[here, :], wq[...], 1, 1)
        tokens_grad[here, :] = grad.astype(bf16)
    scatter.finish()


def run_backward(grid, length_of, qkv, context, dcontext, lse, tokens, first_grad, wq, big, small, sizes):
    length, width = tokens.shape
    dd, du, do = big
    rows = {k: w.shape[0] // grid.count for k, w in (("d", dd), ("u", du), ("o", do), ("q", wq))}
    columns = {k: w.shape[1] for k, w in (("d", dd), ("u", du), ("o", do), ("q", wq))}
    pad = -(-max(sizes) // LANES) * LANES
    shapes = {k: (rows[k], columns[k]) for k in rows}
    shapes["s"] = pad
    plan = scatter_plan(grid, shapes)
    bufs = []
    for name, _, order, r, c in plan:
        bufs += scatter_buffers(grid, order, r, c, f32 if name == "s" else bf16)
    vmem, anywhere = pl.BlockSpec(memory_space=pltpu.VMEM), pl.BlockSpec(memory_space=pl.ANY)
    return pl.pallas_call(
        functools.partial(backward_kernel, grid, plan, sizes),
        out_shape=[jax.ShapeDtypeStruct(shapes[k], f32) for k in ("q", "o", "u", "d")]
        + [jax.ShapeDtypeStruct((16, pad), f32), jax.ShapeDtypeStruct((length, width), bf16)],
        in_specs=[pl.BlockSpec(memory_space=pltpu.SMEM), anywhere] + [vmem] * (9 + len(small)),
        out_specs=[vmem] * 6,
        scratch_shapes=[
            pltpu.VMEM(qkv.shape, bf16),
            pltpu.VMEM(grid.shape + shapes["q"], bf16),
            pltpu.VMEM(grid.shape + (16, pad), f32),
            pltpu.VMEM((2, 7, length, LANES), bf16),
            pltpu.VMEM((2, LANES, length), f32),
            pltpu.SemaphoreType.DMA((len(plan), grid.slots)),
            pltpu.SemaphoreType.DMA((len(plan), grid.slots)),
            pltpu.SemaphoreType.DMA,
        ]
        + bufs,
        compiler_params=pltpu.CompilerParams(
            collective_id=2, has_side_effects=True, vmem_limit_bytes=VMEM_LIMIT
        ),
        name="attend_back_and_scatter",
    )(
        length_of,
        qkv,
        context,
        dcontext,
        lse,
        tokens,
        first_grad,
        wq,
        *[w.reshape(grid.shape + (-1, w.shape[1])) for w in (dd, du, do)],
        *[v.reshape(1, -1) for v in small],
    )


def layer_norm(values, gain, shift):
    center = values - jnp.mean(values, axis=-1, keepdims=True)
    spread = jnp.mean(center * center, axis=-1, keepdims=True)
    return center * lax.rsqrt(spread + eps_norm) * gain + shift


def gelu_exact(values):
    return 0.5 * values * (1.0 + lax.erf(values * (1.0 / math.sqrt(2.0))))


def contrast_loss(pooled, partners):
    unit = pooled * lax.rsqrt(jnp.sum(pooled * pooled, axis=1, keepdims=True) + 1e-06)
    sims = jnp.dot(unit, unit.T, precision=lax.Precision.HIGHEST) / logit_divisor
    columns = jnp.arange(pooled.shape[0], dtype=jnp.int32)
    others = jnp.where(columns[:, None] == columns[None, :], neg_fill, sims)
    row_max = jnp.max(others, axis=1, keepdims=True)
    log_total = row_max[:, 0] + jnp.log(jnp.sum(jnp.exp(others - row_max), axis=1))
    target = jnp.sum(jnp.where(partners[:, None] == columns[None, :], sims, 0.0), axis=1)
    return jnp.mean(log_total - target)


def dot(a, b):
    return jnp.dot(a, b, preferred_element_type=f32)


def on_device(whole, grid, tokens, lengths, keep_attn, keep_ffn, partners, out_cot, *weights):
    (w_qkv, b_qv, w_out, b_out, ln1_gain, ln1_bias, w_up, b_up, w_down, b_down, ln2_gain, ln2_bias, w_pool, b_pool) = weights
    _, length, width = tokens.shape
    big = [w_qkv, w_out, w_up, w_down, w_pool]
    small = [b_qv, b_out, ln1_gain, ln1_bias, b_up, b_down, ln2_gain, ln2_bias, b_pool]
    shard_rows = w_qkv.shape[0]
    if not grid.with_fsdp:
        big = [lax.all_gather(w, "fsdp", axis=0, tiled=True) for w in big]
        small = [lax.all_gather(v, "fsdp", axis=0, tiled=True) for v in small]
    sizes = [v.shape[0] for v in small]
    rows = tokens.reshape(length, width)
    gathered, qkv, context, lse, vectors = run_forward(grid, lengths, rows, big, small)
    wq, wo, wu, wd, wp = gathered
    v_bout, v_g1, v_b1, v_bup, v_bdown, v_g2, v_b2, v_bpool = vectors[1:]
    keep_a = keep_attn.reshape(length, width).astype(f32) * keep_scale
    keep_f = keep_ffn.reshape(length, width).astype(f32) * keep_scale
    attended = dot(context, wo) + v_bout
    first_sum = rows.astype(f32) + attended * keep_a
    hidden = layer_norm(first_sum, v_g1, v_b1)
    hidden_low = hidden.astype(bf16)
    up_pre = dot(hidden_low, wu) + v_bup
    activated = gelu_exact(up_pre).astype(bf16)
    second_sum = hidden + (dot(activated, wd) + v_bdown) * keep_f
    normed = layer_norm(second_sum, v_g2, v_b2)
    layer_out = normed.astype(bf16)
    cls = normed[0:1].astype(bf16)
    pooled = jnp.tanh(dot(cls, wp) + v_bpool)
    pack = jnp.concatenate([pooled, cls.astype(f32), jnp.zeros((6, width), f32)], axis=0)
    everyone = exchange(whole, pack)
    pooled_all, cls_all = everyone[:, 0, :], everyone[:, 1, :].astype(bf16)
    views = pooled_all.shape[0]
    loss, loss_pull = jax.vjp(functools.partial(contrast_loss, partners=partners), pooled_all)
    (pooled_grad,) = loss_pull(jnp.asarray(views, f32))
    pre_all = (pooled_grad * (1.0 - pooled_all * pooled_all)).astype(bf16)
    here = lax.axis_index(AXES)
    pre_grad = lax.dynamic_slice_in_dim(pre_all, here, 1, 0)
    cls_mine = lax.dynamic_slice_in_dim(cls_all, here * shard_rows, shard_rows, 1)
    pool_weight_grad = lax.dot_general(cls_mine, pre_all, (((0,), (0,)), ((), ())), preferred_element_type=f32)
    pool_bias_all = jnp.sum(pre_all.astype(f32), axis=0)
    pool_bias_grad = lax.dynamic_slice_in_dim(pool_bias_all, here * shard_rows, shard_rows, 0)
    cls_grad = lax.dot_general(pre_grad, wp, (((1,), (1,)), ((), ())), preferred_element_type=f32)
    first_row = jnp.arange(length, dtype=jnp.int32)[:, None] == 0
    out_grad = out_cot.reshape(length, width).astype(f32) + jnp.where(first_row, cls_grad, 0.0)
    _, norm_pull = jax.vjp(layer_norm, second_sum, v_g2, v_b2)
    second_grad, g2_grad, b2_grad = norm_pull(out_grad)
    down_grad = (second_grad * keep_f).astype(bf16)
    down_weight_grad = dot(activated.T, down_grad).astype(bf16)
    _, gelu_pull = jax.vjp(gelu_exact, up_pre)
    (up_grad,) = gelu_pull(lax.dot_general(down_grad, wd, (((1,), (1,)), ((), ())), preferred_element_type=f32))
    up_grad = up_grad.astype(bf16)
    up_weight_grad = dot(hidden_low.T, up_grad).astype(bf16)
    hidden_grad = second_grad + lax.dot_general(up_grad, wu, (((1,), (1,)), ((), ())), preferred_element_type=f32)
    _, first_pull = jax.vjp(layer_norm, first_sum, v_g1, v_b1)
    first_grad, g1_grad, b1_grad = first_pull(hidden_grad)
    attended_grad = (first_grad * keep_a).astype(bf16)
    out_weight_grad = dot(context.T, attended_grad).astype(bf16)
    context_grad = lax.dot_general(attended_grad, wo, (((1,), (1,)), ((), ())), preferred_element_type=f32).astype(bf16)

    def column_sum(x):
        return jnp.sum(x.astype(f32), axis=0)

    vector_grads = [column_sum(attended_grad), g1_grad, b1_grad, column_sum(up_grad), column_sum(down_grad), g2_grad, b2_grad]
    rq, ro, ru, rd, rs, tokens_grad = run_backward(
        grid, lengths, qkv, context, context_grad, lse, rows, first_grad, wq,
        [down_weight_grad, up_weight_grad, out_weight_grad], vector_grads, sizes[:-1],
    )
    owned = [rq, ro, ru, rd] + [rs[j, :n] for j, n in enumerate(sizes[:-1])]
    if not grid.with_fsdp:
        owned = [lax.psum_scatter(g, "fsdp", scatter_dimension=0, tiled=True) for g in owned]
    rq, ro, ru, rd, s_qv, s_out, s_g1, s_b1, s_up, s_down, s_g2, s_b2 = owned
    return (
        layer_out.reshape(tokens.shape), tokens_grad.reshape(tokens.shape), rq, s_qv, ro, s_out, s_g1, s_b1, ru, s_up,
        rd, s_down, s_g2, s_b2, pool_weight_grad, pool_bias_grad, loss,
    )


def solution(mesh):
    rows, vector, matrix = P(AXES, None, None), P(AXES), P(AXES, None)
    weights = (matrix, vector, matrix, vector, vector, vector, matrix, vector, matrix, vector, vector, vector, matrix, vector)
    devices = mesh.shape["dp"] * mesh.shape["fsdp"]

    def step(*args):
        whole = Grid(mesh)
        grid = whole if (args[6].shape[0] // devices) % 8 == 0 else Grid(mesh, False)
        return jax.shard_map(
            functools.partial(on_device, whole, grid),
            mesh=mesh,
            in_specs=(rows, vector, rows, rows, P(), rows) + weights,
            out_specs=(rows, rows) + weights + (P(),),
            check_vma=False,
        )(*args)

    return step
```

time: 1070 us -> 319 us (0.30)
  waiting for transfers between devices: 326 us -> 0 us
  matrix products: 332 us -> 65.4 us
  Pallas kernels: 0 us -> 207 us
  blocking collectives: 149 us -> 0 us
  other arithmetic: 166 us -> 19.7 us
  local copies, waits for them, and re-layouts: 72.7 us -> 17.8 us
  between operations: 17.4 us -> 3.78 us
    reduce_scatter x4 -> x0, waiting for transfers between devices: 283 us -> none  [the longest x1 142 us: on_device(): lax.psum_scatter(up_weight_grad, ('dp', 'fsdp'), scatter_dimension=0, til...]
    dot_general x38 -> x15, matrix products: 332 us -> 65.4 us  [the longest x7 38.4 us: dot(): return jnp.dot(a, b, preferred_element_type=f32)]
    pallas_call x0 -> x3, Pallas kernels: none -> 207 us  [the longest x1 98.8 us: run_backward(): pl.pallas_call(functools.partial(backward_kernel, grid, plan, sizes), out...]
    unnamed x2 -> x0, blocking collectives: 81.6 us -> none
    all_gather x1 -> x0, blocking collectives: 66.9 us -> none  [on_device(): lax.all_gather(forward_state['pooled'], ('dp', 'fsdp'), axis=0, tiled=True)]
    sub x2 -> x0, other arithmetic: 60.1 us -> none  [per_block(): shifted = jnp.exp(scores - row_max)]
    convert_element_type x12 -> x2, other arithmetic: 53.8 us -> 0.55 us  [the longest x1 0.55 us: on_device(): layer_out = normed.astype(bf16)]
    unnamed x11 -> x0, waiting for transfers between devices: 38.5 us -> none
  transfers between devices with their start and end apart: 10 -> 0, of which waited for: 4 -> 0; matrix products, arithmetic and copies ran while one was open for 48% -> 0% of each run, Pallas kernels for 0% -> 0%
where the time goes in v1:
time: 319 us; the launch traced here: 313 us
  Pallas kernels  207 us (65%)
  matrix products  65.4 us (21%)
  other arithmetic  19.7 us (6%)
  local copies, waits for them, and re-layouts  17.8 us (6%)
  between operations  3.78 us (1%)
    pallas_call x1, Pallas kernels, run_backward(): pl.pallas_call(functools.partial(backward_kernel, grid, plan, sizes), out...  98.8 us
    pallas_call x1, Pallas kernels, run_forward(): pl.pallas_call(functools.partial(forward_kernel, grid, plan, sizes), out_...  91.4 us
    dot_general x7, matrix products, dot(): return jnp.dot(a, b, preferred_element_type=f32)  38.4 us
    pallas_call x1, Pallas kernels, exchange(): pl.pallas_call(functools.partial(exchange_kernel, grid), out_shape=jax.Sh...  16.5 us
    dot_general x1, matrix products, on_device(): lax.dot_general(down_grad, wd, (((1,), (1,)), ((), ())), preferred_elemen...  14.9 us
    unnamed x65, local copies, waits for them, and re-layouts  6.61 us

profile of v1, /device:TPU:0, one launch (start us, length us, event | category | flops | bytes accessed | tf_op | source)
XLA Modules:
  0.0 313.4 jit_solution(375627168124666211)
XLA Ops:
  2.5 91.4 %gather_and_attend.1 = (bf16[4,2,2,2,24,2304]{5,4,3,2,1,0:T(8,128)(2,1)}, bf16[4,2,2,2,24,768]{5,4,3,2,1,0:T(8,128)(2,1)}, bf16[4,2,2,2,24,3072]{5,4,3,2,1,0:T(8...) custom-call(s32[1]{0:T(128)S(6)} %copy.68.len_ref, ...), custom_call_target="tpu_custom_call" | custom-call | tf_op jit(solution)/shard_map/gather_and_attend/pallas_call | solution.py:371
  98.1 5.0 %fusion.40 = (f32[1024]{0:T(1024)S(1)}, f32[1024,768]{1,0:T(8,128)S(1)}) fusion(s32[1,1024,768]{2,1,0:T(8,128)} %param.22, f32[768]{0:T(1024)S(1)} %reduce, bf16[1024,768]{1,0:T(8,128)(2,1)} %get-tuple-element.39.context, bf16[768,768]{1,0:T(8,128)(2,1)} %bitcast.126, bf16[1,1024,768]{2,1,0:T(8,128)(2,1)} %param.20), kind=kOutput, calls=%fused_computation.107 | convolution fusion | flops 1213463552 | bytes 10624000 | tf_op jit(solution)/shard_map/dot_general | solution.py:621
  103.8 9.5 %multiply_convert_fusion = (bf16[1024,3072]{1,0:T(8,128)(2,1)S(1)}, f32[1024,3072]{1,0:T(8,128)}) fusion(f32[3072]{0:T(1024)S(1)} %bitcast.151, bf16[768,3072]{1,0:T(8,128)(2,1)S(1)} %bitcast.141, f32[1024,768]{1,0:T(8,128)S(1)} %get-tuple-element.88, f32[768]{0:T(1024)S(1)} %reduce.2, f32[768]{0:T(1024)S(1)} %reduce.1, f32[1024]{0:T(1024)S(1)} %fusion.25, ...), kind=kOutput, calls=%fused_computation.2 | convolution fusion | flops 4854644736 | bytes 26765312 | tf_op jit(solution)/shard_map/dot_general | solution.py:621
  113.4 5.7 %fusion.41 = (f32[1024]{0:T(1024)S(1)}, f32[1024,768]{1,0:T(8,128)S(1)}) fusion(s32[1,1024,768]{2,1,0:T(8,128)S(1)} %copy-done.6, f32[768]{0:T(1024)S(1)} %reduce.3, bf16[1024,3072]{1,0:T(8,128)(2,1)S(1)} %get-tuple-element.89, bf16[3072,768]{1,0:T(8,128)(2,1)S(1)} %bitcast.147, f32[768]{0:T(1024)S(1)} %reduce.2, f32[768]{0:T(1024)S(1)} %reduce.1, ...), kind=kOutput, calls=%fused_computation.108 | convolution fusion | flops 4839701504 | bytes 20468736 | tf_op jit(solution)/shard_map/dot_general | solution.py:621
  121.8 16.5 %exchange.1 = f32[4,2,2,2,8,768]{5,4,3,2,1,0:T(8,128)} custom-call(f32[8,768]{1,0:T(8,128)} %maximum_maximum_fusion.row_ref), custom_call_target="tpu_custom_call" | custom-call | tf_op jit(solution)/shard_map/exchange/pallas_call | solution.py:408
  138.4 1.2 slice.47
  139.7 1.3 broadcast_multiply_fusion
  140.9 1.2 slice.48
  144.8 1.7 convolution_reduce_fusion
  147.1 2.8 multiply_reduce_fusion
  151.9 1.7 fusion.61
  153.6 1.7 fusion.39
  156.3 14.9 %convert_reduce_fusion = (f32[3072]{0:T(1024)}, bf16[1024,3072]{1,0:T(8,128)(2,1)}) fusion(bf16[1024,768]{1,0:T(8,128)(2,1)S(1)} %get-tuple-element.73, bf16[3072,768]{1,0:T(8,128)(2,1)S(1)} %bitcast.150, f32[1024,3072]{1,0:T(8,128)} %get-tuple-element.90, f32[3072]{0:T(1024)S(1)} %bitcast.152), kind=kOutput, calls=%fused_computation | convolution fusion | flops 4882166784 | bytes 25190400 | tf_op jit(solution)/shard_map/dot_general | solution.py:672
  171.2 7.1 %convolution_convert_fusion.1 = bf16[3072,768]{1,0:T(8,128)(2,1)} fusion(bf16[1024,3072]{1,0:T(8,128)(2,1)S(1)} %bitcast.154, bf16[1024,768]{1,0:T(8,128)(2,1)S(1)} %get-tuple-element.73), kind=kOutput, calls=%fused_computation.5 | convolution fusion | flops 4834197504 | bytes 12582912 | tf_op jit(solution)/shard_map/dot_general | solution.py:621
  178.9 6.1 %multiply_reduce_fusion.1 = (f32[768]{0:T(1024)S(1)}, f32[1024]{0:T(1024)S(1)}, f32[768]{0:T(1024)S(1)}, f32[1024,768]{1,0:T(8,128)S(1)}) fusion(f32[1024,768]{1,0:T(8,128)S(1)} %copy-done.1, f32[1024]{0:T(1024)S(1)} %fusion.25, f32[1024]{0:T(1024)S(1)} %broadcast_multiply_fusion.2, f32[768]{0:T(1024)S(1)} %reduce.1, bf16[1024,3072]{1,0:T(8,128)(2,1)S(1)} %copy-done.18, ...), kind=kOutput, calls=%fused_computation.19 | convolution fusion | flops 4839699456 | bytes 20472832 | tf_op jit(solution)/shard_map/dot_general | solution.py:675
  185.6 1.4 fusion.38
  187.1 8.3 %convolution_convert_fusion = bf16[768,3072]{1,0:T(8,128)(2,1)} fusion(bf16[1024,3072]{1,0:T(8,128)(2,1)S(1)} %copy-done.18, f32[1024,768]{1,0:T(8,128)S(1)} %copy-done.1, f32[768]{0:T(1024)S(1)} %reduce.2, f32[768]{0:T(1024)S(1)} %reduce.1, f32[1024]{0:T(1024)S(1)} %fusion.25, f32[1024]{0:T(1024)S(1)} %broadcast_multiply_fusion.2), kind=kOutput, calls=%fused_computation.4 | convolution fusion | flops 4838129664 | bytes 14170112 | tf_op jit(solution)/shard_map/dot_general | solution.py:621
  195.9 2.3 convert_reduce_fusion.2
  198.7 2.6 convolution_convert_fusion.2.dcontext
  201.3 2.6 convolution_convert_fusion.3
  203.9 98.8 %attend_back_and_scatter.1 = (f32[24,2304]{1,0:T(8,128)}, f32[24,768]{1,0:T(8,128)}, f32[24,3072]{1,0:T(8,128)}, f32[96,768]{1,0:T(8,128)}, f32[16,128]{1,0:T(8,128)}, /*index=5*/bf16[1024,768]{1,0:T(8,128)(2,1)}) custom-call(s32[1]{0:T(128)S(6)} %copy.68.len_ref, bf16[1024,2304]{1,0:T(8,128)(2,1)} %get-tuple-element.50.qkv_hbm, ...), custom_call_target="tpu_custom_call" | custom-call | tf_op jit(solution)/shard_map/attend_back_and_scatter/pallas_call | solution.py:564
  302.8 1.3 slice_bitcast_fusion.3
  305.2 1.4 slice_bitcast_fusion
  306.6 2.7 copy.69
  (115 shorter events, 20.6 us)
Async XLA Ops:
  97.3 6.4 %slice-start = ((s8[4718592]{0:T(1024)(128)(4,1)}), s8[524288]{0:T(1024)(128)(4,1)S(1)}, s32[]{:S(2)}) async-start(s8[4718592]{0:T(1024)(128)(4,1)} %bitcast.139), calls=%async_computation | async-start | bytes 1048576
  98.1 5.6 %slice-start.1 = ((s8[4718592]{0:T(1024)(128)(4,1)}), s8[4194304]{0:T(1024)(128)(4,1)S(1)}, s32[]{:S(2)}) async-start(s8[4718592]{0:T(1024)(128)(4,1)} %bitcast.139), calls=%async_computation.1 | async-start | bytes 8388608
  103.1 10.3 %copy-start = (f32[1024,768]{1,0:T(8,128)}, f32[1024,768]{1,0:T(8,128)S(1)}, u32[]{:S(2)}) copy-start(f32[1024,768]{1,0:T(8,128)S(1)} %get-tuple-element.88) | copy-start | bytes 9437188
  103.1 10.3 %slice-start.4 = ((s8[4718592]{0:T(1024)(128)(4,1)}), s8[4194304]{0:T(1024)(128)(4,1)S(1)}, s32[]{:S(2)}) async-start(s8[4718592]{0:T(1024)(128)(4,1)} %bitcast.145), calls=%async_computation.4 | async-start | bytes 8388608
  103.8 9.6 %copy-start.6 = (s32[1,1024,768]{2,1,0:T(8,128)S(1)}, s32[1,1024,768]{2,1,0:T(8,128)}, u32[]{:S(2)}) copy-start(s32[1,1024,768]{2,1,0:T(8,128)} %param.23) | copy-start | bytes 9437188
  103.8 9.6 %slice-start.5 = ((s8[4718592]{0:T(1024)(128)(4,1)}), s8[524288]{0:T(1024)(128)(4,1)S(1)}, s32[]{:S(2)}) async-start(s8[4718592]{0:T(1024)(128)(4,1)} %bitcast.145), calls=%async_computation.5 | async-start | bytes 1048576
  113.4 5.7 %copy-start.19 = (bf16[1024,3072]{1,0:T(8,128)(2,1)}, bf16[1024,3072]{1,0:T(8,128)(2,1)S(1)}, u32[]{:S(2)}) copy-start(bf16[1024,3072]{1,0:T(8,128)(2,1)S(1)} %get-tuple-element.89) | copy-start | bytes 18874372
  119.6 23.0 %copy-start.13 = (s32[32]{0:T(128)S(1)}, s32[32]{0:T(128)}, u32[]{:S(2)}) copy-start(s32[32]{0:T(128)} %param.24) | copy-start | bytes 388
  120.8 26.3 %copy-start.14 = (pred[1024]{0:T(1024)(128)(4,1)S(1)}, pred[1024]{0:T(1024)(128)(4,1)}, u32[]{:S(2)}) copy-start(pred[1024]{0:T(1024)(128)(4,1)} %iota_compare_fusion.2) | copy-start | bytes 3076
  149.9 3.7 %copy-start.4 = (bf16[1,1024,768]{2,1,0:T(8,128)(2,1)S(1)}, bf16[1,1024,768]{2,1,0:T(8,128)(2,1)}, u32[]{:S(2)}) copy-start(bf16[1,1024,768]{2,1,0:T(8,128)(2,1)} %param.25) | copy-start | bytes 4718596
  151.9 4.3 %slice-start.6 = ((s8[4718592]{0:T(1024)(128)(4,1)}), s8[4194304]{0:T(1024)(128)(4,1)S(1)}, s32[]{:S(2)}) async-start(s8[4718592]{0:T(1024)(128)(4,1)} %bitcast.148), calls=%async_computation.6 | async-start | bytes 8388608
  153.6 2.7 slice-start.7
  155.6 15.6 %slice-start.8 = ((s8[6291456]{0:T(1024)(128)(4,1)}), s8[4194304]{0:T(1024)(128)(4,1)S(1)}, s32[]{:S(2)}) async-start(s8[6291456]{0:T(1024)(128)(4,1)} %bitcast.153), calls=%async_computation.8 | async-start | bytes 8388608
  155.6 23.3 %slice-start.2 = ((s8[4718592]{0:T(1024)(128)(4,1)}), s8[524288]{0:T(1024)(128)(4,1)S(1)}, s32[]{:S(2)}) async-start(s8[4718592]{0:T(1024)(128)(4,1)} %bitcast.142), calls=%async_computation.2 | async-start | bytes 1048576
  156.3 14.9 %slice-start.9 = ((s8[6291456]{0:T(1024)(128)(4,1)}), s8[2097152]{0:T(1024)(128)(4,1)S(1)}, s32[]{:S(2)}) async-start(s8[6291456]{0:T(1024)(128)(4,1)} %bitcast.153), calls=%async_computation.9 | async-start | bytes 4194304
  156.3 22.6 %slice-start.3 = ((s8[4718592]{0:T(1024)(128)(4,1)}), s8[4194304]{0:T(1024)(128)(4,1)S(1)}, s32[]{:S(2)}) async-start(s8[4718592]{0:T(1024)(128)(4,1)} %bitcast.142), calls=%async_computation.3 | async-start | bytes 8388608
  171.2 7.7 %copy-start.1 = (f32[1024,768]{1,0:T(8,128)S(1)}, f32[1024,768]{1,0:T(8,128)}, u32[]{:S(2)}) copy-start(f32[1024,768]{1,0:T(8,128)} %copy-done) | copy-start | bytes 9437188
  171.2 7.7 %copy-start.18 = (bf16[1024,3072]{1,0:T(8,128)(2,1)S(1)}, bf16[1024,3072]{1,0:T(8,128)(2,1)}, u32[]{:S(2)}) copy-start(bf16[1024,3072]{1,0:T(8,128)(2,1)} %get-tuple-element.99) | copy-start | bytes 18874372
  187.0 8.9 %copy-start.2 = (s32[1,1024,768]{2,1,0:T(8,128)S(1)}, s32[1,1024,768]{2,1,0:T(8,128)}, u32[]{:S(2)}) copy-start(s32[1,1024,768]{2,1,0:T(8,128)} %param.22) | copy-start | bytes 9437188
  195.9 2.8 copy-start.8
  302.7 6.6 %copy-start.11 = (f32[24,2304]{1,0:T(8,128)S(1)}, f32[24,2304]{1,0:T(8,128)}, u32[]{:S(2)}) copy-start(f32[24,2304]{1,0:T(8,128)} %get-tuple-element.121) | copy-start | bytes 663556
  302.7 7.2 %copy-start.12 = (f32[24,768]{1,0:T(8,128)S(1)}, f32[24,768]{1,0:T(8,128)}, u32[]{:S(2)}) copy-start(f32[24,768]{1,0:T(8,128)} %get-tuple-element.123) | copy-start | bytes 221188
  302.7 7.9 %copy-start.10 = (f32[24,3072]{1,0:T(8,128)S(1)}, f32[24,3072]{1,0:T(8,128)}, u32[]{:S(2)}) copy-start(f32[24,3072]{1,0:T(8,128)} %get-tuple-element.127) | copy-start | bytes 884740
  302.8 8.6 %copy-start.9 = (f32[96,768]{1,0:T(8,128)S(1)}, f32[96,768]{1,0:T(8,128)}, u32[]{:S(2)}) copy-start(f32[96,768]{1,0:T(8,128)} %get-tuple-element.129) | copy-start | bytes 884740
  (6 other events, 9.4 us)
